TPU v7x, 32 devices: a whole 2x2x4 slice. The times are simulated.
32 devices in a mesh: blk: 16 (over z, x, core), narrow: 2 (over y).
Axes of the slice: x: 2, y: 2, z: 4, core: 2. Of those that a mesh axis runs over, the one named last changes fastest.
Arguments:
- rhs: float32 [6144, 256], P('blk', 'narrow'), may hold values from -6 to 6
- zo: float32 [6144, 64], P('blk'), may hold values from -0.109375 to 0.109375
- e_diag: float32 [64, 96, 96], P('blk'), may hold values from -0.18 to 0.18
- a_off: float32 [64, 3, 96, 96], P('blk'), may hold values from -0.18 to 0.18
- e_off: float32 [64, 3, 96, 96], P('blk'), may hold values from -0.09 to 0.09
- col_index: int32 [64, 3], P('blk'), may hold values from 0 to 63, as said below
- inv_diag: float32 [2, 64, 96, 96], P(None, 'blk'), may hold values from -0.625 to 0.625
- shifts: float32 [2], replicated, may hold values from 0.5 to 2
Outputs:
- residual: float32 [6144, 256], P('blk', 'narrow')
- cross: float32 [64, 2, 256], P(('blk', 'narrow'))
Inputs may be any that keep to these rules, and one draw needn't show every extreme that they name: `col_index`: each block column index differs from its own block row by 1 or 2 in either direction, near the ends of the range reflected to the other side; the three indices of a row may repeat.
All inputs are finite; a program needn't handle non-finite values.
Results may differ from a plain program's by a relative error of at most 0.0001.
Values sent between devices are 32-bit elements; how exact they have to be, the bound alone decides.
A program may use at most 64 MiB of HBM per device.

v0:
```python
import jax
import jax.numpy as jnp
from jax import lax
from jax.sharding import PartitionSpec as P

SWEEPS = 8


precise = lax.Precision.HIGHEST


def extended_2(cells, sides, width):
    for axis, dim in sides:
        count = lax.axis_size(axis)
        ends = count - 1
        head = lax.slice_in_dim(cells, 0, width, axis=dim)
        tail = lax.slice_in_dim(cells, cells.shape[dim] - width, cells.shape[dim], axis=dim)
        cells = jnp.concatenate(
            [
                lax.ppermute(tail, axis, [(i, (i + 1) % count) for i in range(ends)]),
                cells,
                lax.ppermute(head, axis, [((i + 1) % count, i) for i in range(ends)]),
            ],
            axis=dim,
        )
    return cells


def block_product(matrices, field):
    return jnp.einsum("nab,nbk->nak", matrices, field, precision=precise)


def shards(rhs, zo, e_diag, a_off, e_off, col_index, inv_diag, shifts):
    row_count, col_width = rhs.shape
    blocks = e_diag.shape[0]
    block_size = e_diag.shape[1]
    local_col = col_index - lax.axis_index("blk") * blocks + 2

    def coupled(coupling, field):
        padded = extended_2(field.reshape(row_count, col_width), (("blk", 0),), 2 * block_size)
        extended = padded.reshape(blocks + 4, block_size, col_width)
        picked = jnp.take(extended, local_col, axis=0)
        return jnp.einsum("nsab,nsbk->nak", coupling, picked, precision=precise)

    current = rhs.reshape(blocks, block_size, col_width)
    images = []
    for which in range(2):
        shift_value = shifts[which]
        coupling = a_off - shift_value * e_off
        inverse = inv_diag[which]
        iterate = block_product(inverse, current)
        for sweep in range(SWEEPS):
            iterate = block_product(inverse, current - coupled(coupling, iterate))
        mass_image = block_product(e_diag, iterate) + coupled(e_off, iterate)
        current = current + 2.0 * shift_value * mass_image
        images.append(jnp.sqrt(2.0 * shift_value) * mass_image)
    stacked = jnp.stack(images, axis=2).reshape(row_count, 2, col_width)
    summed = lax.psum_scatter(
        jnp.einsum("ro,rsk->osk", zo, stacked, precision=precise),
        "blk",
        scatter_dimension=0,
        tiled=True,
    )
    cross = lax.all_to_all(summed, "narrow", split_axis=0, concat_axis=2, tiled=True)
    return (current.reshape(row_count, col_width), cross)


def solution(mesh):
    placed = (
        P("blk", "narrow"),
        P("blk", None),
        P("blk", None, None),
        P("blk", None, None, None),
        P("blk", None, None, None),
        P("blk", None),
        P(None, "blk", None, None),
        P(),
    )
    return jax.shard_map(
        shards,
        mesh=mesh,
        in_specs=placed,
        out_specs=(P("blk", "narrow"), P(("blk", "narrow"), None, None)),
        check_vma=False,
    )
```

profile of v0, /device:TPU:0, one launch (start us, length us, event | category | flops | bytes accessed | tf_op | source)
XLA Modules:
  0.0 327.6 jit_solution(1364033609867359985)
XLA Ops:
  8.7 2.4 collective-permute-start
  14.3 2.5 multiply_subtract_fusion
  20.6 5.1 %collective-permute-start.2 = (f32[192,128]{1,0:T(8,128)S(1)}, f32[192,128]{1,0:T(8,128)S(1)}, u32[]{:S(2)}, u32[]{:S(2)}) collective-permute-start(f32[192,128]{1,0:T(8,128)S(1)} %bitcast.421), channel_id=1, source_target_pairs={{0,2},{2,4},{4,6},{6,8},{8,10},{10,12},{12,14},{14,16},{16,18},{18... | collective-permute-start | bytes 294920 | tf_op jit(solution)/shard_map/ppermute | solution.py:20
  27.0 3.1 collective-permute-done.3
  33.1 5.1 %collective-permute-start.4 = (f32[192,128]{1,0:T(8,128)S(1)}, f32[192,128]{1,0:T(8,128)S(1)}, u32[]{:S(2)}, u32[]{:S(2)}) collective-permute-start(f32[192,128]{1,0:T(8,128)S(1)} %bitcast.422), channel_id=1, source_target_pairs={{0,2},{2,4},{4,6},{6,8},{8,10},{10,12},{12,14},{14,16},{16,18},{18... | collective-permute-start | bytes 294920 | tf_op jit(solution)/shard_map/ppermute | solution.py:20
  39.6 1.9 collective-permute-done.5
  44.4 6.4 %collective-permute-start.6 = (f32[192,128]{1,0:T(8,128)S(1)}, f32[192,128]{1,0:T(8,128)S(1)}, u32[]{:S(2)}, u32[]{:S(2)}) collective-permute-start(f32[192,128]{1,0:T(8,128)S(1)} %bitcast.423), channel_id=1, source_target_pairs={{0,2},{2,4},{4,6},{6,8},{8,10},{10,12},{12,14},{14,16},{16,18},{18... | collective-permute-start | bytes 294920 | tf_op jit(solution)/shard_map/ppermute | solution.py:20
  52.1 1.9 collective-permute-done.7
  57.0 5.6 %collective-permute-start.8 = (f32[192,128]{1,0:T(8,128)S(1)}, f32[192,128]{1,0:T(8,128)S(1)}, u32[]{:S(2)}, u32[]{:S(2)}) collective-permute-start(f32[192,128]{1,0:T(8,128)S(1)} %bitcast.424), channel_id=1, source_target_pairs={{0,2},{2,4},{4,6},{6,8},{8,10},{10,12},{12,14},{14,16},{16,18},{18... | collective-permute-start | bytes 294920 | tf_op jit(solution)/shard_map/ppermute | solution.py:20
  63.8 1.9 collective-permute-done.9
  68.7 5.6 %collective-permute-start.10 = (f32[192,128]{1,0:T(8,128)S(1)}, f32[192,128]{1,0:T(8,128)S(1)}, u32[]{:S(2)}, u32[]{:S(2)}) collective-permute-start(f32[192,128]{1,0:T(8,128)S(1)} %bitcast.425), channel_id=1, source_target_pairs={{0,2},{2,4},{4,6},{6,8},{8,10},{10,12},{12,14},{14,16},{16,18},{18... | collective-permute-start | bytes 294920 | tf_op jit(solution)/shard_map/ppermute | solution.py:20
  75.6 1.9 collective-permute-done.11
  80.4 5.6 %collective-permute-start.12 = (f32[192,128]{1,0:T(8,128)S(1)}, f32[192,128]{1,0:T(8,128)S(1)}, u32[]{:S(2)}, u32[]{:S(2)}) collective-permute-start(f32[192,128]{1,0:T(8,128)S(1)} %bitcast.426), channel_id=1, source_target_pairs={{0,2},{2,4},{4,6},{6,8},{8,10},{10,12},{12,14},{14,16},{16,18},{18... | collective-permute-start | bytes 294920 | tf_op jit(solution)/shard_map/ppermute | solution.py:20
  87.3 1.9 collective-permute-done.13
  92.2 5.6 %collective-permute-start.14 = (f32[192,128]{1,0:T(8,128)S(1)}, f32[192,128]{1,0:T(8,128)S(1)}, u32[]{:S(2)}, u32[]{:S(2)}) collective-permute-start(f32[192,128]{1,0:T(8,128)S(1)} %bitcast.427), channel_id=1, source_target_pairs={{0,2},{2,4},{4,6},{6,8},{8,10},{10,12},{12,14},{14,16},{16,18},{18... | collective-permute-start | bytes 294920 | tf_op jit(solution)/shard_map/ppermute | solution.py:20
  103.9 5.6 %collective-permute-start.16 = (f32[192,128]{1,0:T(8,128)S(1)}, f32[192,128]{1,0:T(8,128)S(1)}, u32[]{:S(2)}, u32[]{:S(2)}) collective-permute-start(f32[192,128]{1,0:T(8,128)S(1)} %bitcast.420), channel_id=1, source_target_pairs={{0,2},{2,4},{4,6},{6,8},{8,10},{10,12},{12,14},{14,16},{16,18},{18... | collective-permute-start | bytes 294920 | tf_op jit(solution)/shard_map/ppermute | solution.py:20
  116.3 5.6 %collective-permute-start.18 = (f32[192,128]{1,0:T(8,128)S(1)}, f32[192,128]{1,0:T(8,128)S(1)}, u32[]{:S(2)}, u32[]{:S(2)}) collective-permute-start(f32[192,128]{1,0:T(8,128)S(1)} %bitcast.428), channel_id=1, source_target_pairs={{0,2},{2,4},{4,6},{6,8},{8,10},{10,12},{12,14},{14,16},{16,18},{18... | collective-permute-start | bytes 294920 | tf_op jit(solution)/shard_map/ppermute | solution.py:20
  123.1 1.9 collective-permute-done.19
  127.9 5.6 %collective-permute-start.20 = (f32[192,128]{1,0:T(8,128)S(1)}, f32[192,128]{1,0:T(8,128)S(1)}, u32[]{:S(2)}, u32[]{:S(2)}) collective-permute-start(f32[192,128]{1,0:T(8,128)S(1)} %bitcast.429), channel_id=1, source_target_pairs={{0,2},{2,4},{4,6},{6,8},{8,10},{10,12},{12,14},{14,16},{16,18},{18... | collective-permute-start | bytes 294920 | tf_op jit(solution)/shard_map/ppermute | solution.py:20
  134.7 1.9 collective-permute-done.21
  139.6 5.6 %collective-permute-start.22 = (f32[192,128]{1,0:T(8,128)S(1)}, f32[192,128]{1,0:T(8,128)S(1)}, u32[]{:S(2)}, u32[]{:S(2)}) collective-permute-start(f32[192,128]{1,0:T(8,128)S(1)} %bitcast.430), channel_id=1, source_target_pairs={{0,2},{2,4},{4,6},{6,8},{8,10},{10,12},{12,14},{14,16},{16,18},{18... | collective-permute-start | bytes 294920 | tf_op jit(solution)/shard_map/ppermute | solution.py:20
  146.5 1.9 collective-permute-done.23
  151.3 5.6 %collective-permute-start.24 = (f32[192,128]{1,0:T(8,128)S(1)}, f32[192,128]{1,0:T(8,128)S(1)}, u32[]{:S(2)}, u32[]{:S(2)}) collective-permute-start(f32[192,128]{1,0:T(8,128)S(1)} %bitcast.431), channel_id=1, source_target_pairs={{0,2},{2,4},{4,6},{6,8},{8,10},{10,12},{12,14},{14,16},{16,18},{18... | collective-permute-start | bytes 294920 | tf_op jit(solution)/shard_map/ppermute | solution.py:20
  163.1 5.6 %collective-permute-start.26 = (f32[192,128]{1,0:T(8,128)S(1)}, f32[192,128]{1,0:T(8,128)S(1)}, u32[]{:S(2)}, u32[]{:S(2)}) collective-permute-start(f32[192,128]{1,0:T(8,128)S(1)} %bitcast.432), channel_id=1, source_target_pairs={{0,2},{2,4},{4,6},{6,8},{8,10},{10,12},{12,14},{14,16},{16,18},{18... | collective-permute-start | bytes 294920 | tf_op jit(solution)/shard_map/ppermute | solution.py:20
  169.9 1.9 collective-permute-done.27
  174.8 5.6 %collective-permute-start.28 = (f32[192,128]{1,0:T(8,128)S(1)}, f32[192,128]{1,0:T(8,128)S(1)}, u32[]{:S(2)}, u32[]{:S(2)}) collective-permute-start(f32[192,128]{1,0:T(8,128)S(1)} %bitcast.433), channel_id=1, source_target_pairs={{0,2},{2,4},{4,6},{6,8},{8,10},{10,12},{12,14},{14,16},{16,18},{18... | collective-permute-start | bytes 294920 | tf_op jit(solution)/shard_map/ppermute | solution.py:20
  181.7 1.9 collective-permute-done.29
  186.5 5.6 %collective-permute-start.30 = (f32[192,128]{1,0:T(8,128)S(1)}, f32[192,128]{1,0:T(8,128)S(1)}, u32[]{:S(2)}, u32[]{:S(2)}) collective-permute-start(f32[192,128]{1,0:T(8,128)S(1)} %bitcast.434), channel_id=1, source_target_pairs={{0,2},{2,4},{4,6},{6,8},{8,10},{10,12},{12,14},{14,16},{16,18},{18... | collective-permute-start | bytes 294920 | tf_op jit(solution)/shard_map/ppermute | solution.py:20
  198.3 5.6 %collective-permute-start.32 = (f32[192,128]{1,0:T(8,128)S(1)}, f32[192,128]{1,0:T(8,128)S(1)}, u32[]{:S(2)}, u32[]{:S(2)}) collective-permute-start(f32[192,128]{1,0:T(8,128)S(1)} %bitcast.403), channel_id=1, source_target_pairs={{0,2},{2,4},{4,6},{6,8},{8,10},{10,12},{12,14},{14,16},{16,18},{18... | collective-permute-start | bytes 294920 | tf_op jit(solution)/shard_map/ppermute | solution.py:20
  208.9 5.6 %collective-permute-start.34 = (f32[192,128]{1,0:T(8,128)S(1)}, f32[192,128]{1,0:T(8,128)S(1)}, u32[]{:S(2)}, u32[]{:S(2)}) collective-permute-start(f32[192,128]{1,0:T(8,128)S(1)} %bitcast.405), channel_id=1, source_target_pairs={{0,2},{2,4},{4,6},{6,8},{8,10},{10,12},{12,14},{14,16},{16,18},{18... | collective-permute-start | bytes 294920 | tf_op jit(solution)/shard_map/ppermute | solution.py:20
  224.1 89.0 %all-reduce.3.cloned.1.call-done = f32[64,2,128]{2,0,1:T(8,128)} async-done(((f32[64,2,128]{2,0,1:T(8,128)}), f32[64,2,128]{2,0,1:T(8,128)}) %all-reduce.3.cloned.1.call-update) | async-done | bytes 65552
  313.8 6.3 %all_to_all.18 = f32[4,2,128]{2,1,0:T(2,128)S(1)} all-to-all(f32[4,2,128]{2,1,0:T(2,128)S(1)} %copy.11), channel_id=1, replica_groups=mesh['blk'=16,'narrow'=2] {'narrow'}, dimensions={0} | all-to-all | bytes 8192 | tf_op jit(solution)/shard_map/all_to_all | solution.py:64
  (168 shorter events, 93.7 us)
Async XLA Ops:
  7.2 305.9 %all-reduce.3.cloned.1.call-start = ((), (), s32[]{:S(2)}) async-start(), calls=%async_computation.1 | async-start | bytes 131072
  8.7 8.2 %collective-permute-start = (f32[192,128]{1,0:T(8,128)S(1)}, f32[192,128]{1,0:T(8,128)S(1)}, u32[]{:S(2)}, u32[]{:S(2)}) collective-permute-start(f32[192,128]{1,0:T(8,128)S(1)} %bitcast.400), channel_id=1, source_target_pairs={{0,2},{2,4},{4,6},{6,8},{8,10},{10,12},{12,14},{14,16},{16,18},{18... | collective-permute-start | bytes 294920 | tf_op jit(solution)/shard_map/ppermute | solution.py:20
  11.1 5.8 %collective-permute-start.1 = (f32[192,128]{1,0:T(8,128)S(1)}, f32[192,128]{1,0:T(8,128)S(1)}, u32[]{:S(2)}, u32[]{:S(2)}) collective-permute-start(f32[192,128]{1,0:T(8,128)S(1)} %bitcast.399), channel_id=1, source_target_pairs={{2,0},{4,2},{6,4},{8,6},{10,8},{12,10},{14,12},{16,14},{18,16},{20... | collective-permute-start | bytes 294920 | tf_op jit(solution)/shard_map/ppermute | solution.py:22
  20.6 6.4 %collective-permute-start.2 = (f32[192,128]{1,0:T(8,128)S(1)}, f32[192,128]{1,0:T(8,128)S(1)}, u32[]{:S(2)}, u32[]{:S(2)}) collective-permute-start(f32[192,128]{1,0:T(8,128)S(1)} %bitcast.421), channel_id=1, source_target_pairs={{0,2},{2,4},{4,6},{6,8},{8,10},{10,12},{12,14},{14,16},{16,18},{18... | collective-permute-start | bytes 294920 | tf_op jit(solution)/shard_map/ppermute | solution.py:20
  25.7 4.4 %collective-permute-start.3 = (f32[192,128]{1,0:T(8,128)S(1)}, f32[192,128]{1,0:T(8,128)S(1)}, u32[]{:S(2)}, u32[]{:S(2)}) collective-permute-start(f32[192,128]{1,0:T(8,128)S(1)} %bitcast.406), channel_id=1, source_target_pairs={{2,0},{4,2},{6,4},{8,6},{10,8},{12,10},{14,12},{16,14},{18,16},{20... | collective-permute-start | bytes 294920 | tf_op jit(solution)/shard_map/ppermute | solution.py:22
  33.1 6.5 %collective-permute-start.4 = (f32[192,128]{1,0:T(8,128)S(1)}, f32[192,128]{1,0:T(8,128)S(1)}, u32[]{:S(2)}, u32[]{:S(2)}) collective-permute-start(f32[192,128]{1,0:T(8,128)S(1)} %bitcast.422), channel_id=1, source_target_pairs={{0,2},{2,4},{4,6},{6,8},{8,10},{10,12},{12,14},{14,16},{16,18},{18... | collective-permute-start | bytes 294920 | tf_op jit(solution)/shard_map/ppermute | solution.py:20
  38.3 3.2 collective-permute-start.5
  44.4 7.7 %collective-permute-start.6 = (f32[192,128]{1,0:T(8,128)S(1)}, f32[192,128]{1,0:T(8,128)S(1)}, u32[]{:S(2)}, u32[]{:S(2)}) collective-permute-start(f32[192,128]{1,0:T(8,128)S(1)} %bitcast.423), channel_id=1, source_target_pairs={{0,2},{2,4},{4,6},{6,8},{8,10},{10,12},{12,14},{14,16},{16,18},{18... | collective-permute-start | bytes 294920 | tf_op jit(solution)/shard_map/ppermute | solution.py:20
  50.8 3.2 collective-permute-start.7
  57.0 6.9 %collective-permute-start.8 = (f32[192,128]{1,0:T(8,128)S(1)}, f32[192,128]{1,0:T(8,128)S(1)}, u32[]{:S(2)}, u32[]{:S(2)}) collective-permute-start(f32[192,128]{1,0:T(8,128)S(1)} %bitcast.424), channel_id=1, source_target_pairs={{0,2},{2,4},{4,6},{6,8},{8,10},{10,12},{12,14},{14,16},{16,18},{18... | collective-permute-start | bytes 294920 | tf_op jit(solution)/shard_map/ppermute | solution.py:20
  62.5 3.2 collective-permute-start.9
  68.7 6.9 %collective-permute-start.10 = (f32[192,128]{1,0:T(8,128)S(1)}, f32[192,128]{1,0:T(8,128)S(1)}, u32[]{:S(2)}, u32[]{:S(2)}) collective-permute-start(f32[192,128]{1,0:T(8,128)S(1)} %bitcast.425), channel_id=1, source_target_pairs={{0,2},{2,4},{4,6},{6,8},{8,10},{10,12},{12,14},{14,16},{16,18},{18... | collective-permute-start | bytes 294920 | tf_op jit(solution)/shard_map/ppermute | solution.py:20
  74.3 3.2 collective-permute-start.11
  80.4 6.9 %collective-permute-start.12 = (f32[192,128]{1,0:T(8,128)S(1)}, f32[192,128]{1,0:T(8,128)S(1)}, u32[]{:S(2)}, u32[]{:S(2)}) collective-permute-start(f32[192,128]{1,0:T(8,128)S(1)} %bitcast.426), channel_id=1, source_target_pairs={{0,2},{2,4},{4,6},{6,8},{8,10},{10,12},{12,14},{14,16},{16,18},{18... | collective-permute-start | bytes 294920 | tf_op jit(solution)/shard_map/ppermute | solution.py:20
  86.0 3.2 collective-permute-start.13
  92.2 7.1 %collective-permute-start.14 = (f32[192,128]{1,0:T(8,128)S(1)}, f32[192,128]{1,0:T(8,128)S(1)}, u32[]{:S(2)}, u32[]{:S(2)}) collective-permute-start(f32[192,128]{1,0:T(8,128)S(1)} %bitcast.427), channel_id=1, source_target_pairs={{0,2},{2,4},{4,6},{6,8},{8,10},{10,12},{12,14},{14,16},{16,18},{18... | collective-permute-start | bytes 294920 | tf_op jit(solution)/shard_map/ppermute | solution.py:20
  97.7 3.2 collective-permute-start.15
  103.9 7.5 %collective-permute-start.16 = (f32[192,128]{1,0:T(8,128)S(1)}, f32[192,128]{1,0:T(8,128)S(1)}, u32[]{:S(2)}, u32[]{:S(2)}) collective-permute-start(f32[192,128]{1,0:T(8,128)S(1)} %bitcast.420), channel_id=1, source_target_pairs={{0,2},{2,4},{4,6},{6,8},{8,10},{10,12},{12,14},{14,16},{16,18},{18... | collective-permute-start | bytes 294920 | tf_op jit(solution)/shard_map/ppermute | solution.py:20
  109.5 3.2 collective-permute-start.17
  116.3 6.9 %collective-permute-start.18 = (f32[192,128]{1,0:T(8,128)S(1)}, f32[192,128]{1,0:T(8,128)S(1)}, u32[]{:S(2)}, u32[]{:S(2)}) collective-permute-start(f32[192,128]{1,0:T(8,128)S(1)} %bitcast.428), channel_id=1, source_target_pairs={{0,2},{2,4},{4,6},{6,8},{8,10},{10,12},{12,14},{14,16},{16,18},{18... | collective-permute-start | bytes 294920 | tf_op jit(solution)/shard_map/ppermute | solution.py:20
  121.8 3.2 collective-permute-start.19
  127.9 6.9 %collective-permute-start.20 = (f32[192,128]{1,0:T(8,128)S(1)}, f32[192,128]{1,0:T(8,128)S(1)}, u32[]{:S(2)}, u32[]{:S(2)}) collective-permute-start(f32[192,128]{1,0:T(8,128)S(1)} %bitcast.429), channel_id=1, source_target_pairs={{0,2},{2,4},{4,6},{6,8},{8,10},{10,12},{12,14},{14,16},{16,18},{18... | collective-permute-start | bytes 294920 | tf_op jit(solution)/shard_map/ppermute | solution.py:20
  133.4 3.2 collective-permute-start.21
  139.6 6.9 %collective-permute-start.22 = (f32[192,128]{1,0:T(8,128)S(1)}, f32[192,128]{1,0:T(8,128)S(1)}, u32[]{:S(2)}, u32[]{:S(2)}) collective-permute-start(f32[192,128]{1,0:T(8,128)S(1)} %bitcast.430), channel_id=1, source_target_pairs={{0,2},{2,4},{4,6},{6,8},{8,10},{10,12},{12,14},{14,16},{16,18},{18... | collective-permute-start | bytes 294920 | tf_op jit(solution)/shard_map/ppermute | solution.py:20
  145.2 3.2 collective-permute-start.23
  151.3 6.9 %collective-permute-start.24 = (f32[192,128]{1,0:T(8,128)S(1)}, f32[192,128]{1,0:T(8,128)S(1)}, u32[]{:S(2)}, u32[]{:S(2)}) collective-permute-start(f32[192,128]{1,0:T(8,128)S(1)} %bitcast.431), channel_id=1, source_target_pairs={{0,2},{2,4},{4,6},{6,8},{8,10},{10,12},{12,14},{14,16},{16,18},{18... | collective-permute-start | bytes 294920 | tf_op jit(solution)/shard_map/ppermute | solution.py:20
  163.1 6.9 %collective-permute-start.26 = (f32[192,128]{1,0:T(8,128)S(1)}, f32[192,128]{1,0:T(8,128)S(1)}, u32[]{:S(2)}, u32[]{:S(2)}) collective-permute-start(f32[192,128]{1,0:T(8,128)S(1)} %bitcast.432), channel_id=1, source_target_pairs={{0,2},{2,4},{4,6},{6,8},{8,10},{10,12},{12,14},{14,16},{16,18},{18... | collective-permute-start | bytes 294920 | tf_op jit(solution)/shard_map/ppermute | solution.py:20
  174.8 6.9 %collective-permute-start.28 = (f32[192,128]{1,0:T(8,128)S(1)}, f32[192,128]{1,0:T(8,128)S(1)}, u32[]{:S(2)}, u32[]{:S(2)}) collective-permute-start(f32[192,128]{1,0:T(8,128)S(1)} %bitcast.433), channel_id=1, source_target_pairs={{0,2},{2,4},{4,6},{6,8},{8,10},{10,12},{12,14},{14,16},{16,18},{18... | collective-permute-start | bytes 294920 | tf_op jit(solution)/shard_map/ppermute | solution.py:20
  186.5 7.1 %collective-permute-start.30 = (f32[192,128]{1,0:T(8,128)S(1)}, f32[192,128]{1,0:T(8,128)S(1)}, u32[]{:S(2)}, u32[]{:S(2)}) collective-permute-start(f32[192,128]{1,0:T(8,128)S(1)} %bitcast.434), channel_id=1, source_target_pairs={{0,2},{2,4},{4,6},{6,8},{8,10},{10,12},{12,14},{14,16},{16,18},{18... | collective-permute-start | bytes 294920 | tf_op jit(solution)/shard_map/ppermute | solution.py:20
  198.3 7.6 %collective-permute-start.32 = (f32[192,128]{1,0:T(8,128)S(1)}, f32[192,128]{1,0:T(8,128)S(1)}, u32[]{:S(2)}, u32[]{:S(2)}) collective-permute-start(f32[192,128]{1,0:T(8,128)S(1)} %bitcast.403), channel_id=1, source_target_pairs={{0,2},{2,4},{4,6},{6,8},{8,10},{10,12},{12,14},{14,16},{16,18},{18... | collective-permute-start | bytes 294920 | tf_op jit(solution)/shard_map/ppermute | solution.py:20
  208.9 6.9 %collective-permute-start.34 = (f32[192,128]{1,0:T(8,128)S(1)}, f32[192,128]{1,0:T(8,128)S(1)}, u32[]{:S(2)}, u32[]{:S(2)}) collective-permute-start(f32[192,128]{1,0:T(8,128)S(1)} %bitcast.405), channel_id=1, source_target_pairs={{0,2},{2,4},{4,6},{6,8},{8,10},{10,12},{12,14},{14,16},{16,18},{18... | collective-permute-start | bytes 294920 | tf_op jit(solution)/shard_map/ppermute | solution.py:20
  214.5 3.2 collective-permute-start.35
  (15 other events, 137.0 us)
Sparse Core Ops, SparseCore 0:
  222.3 90.7 all-reduce.2
where the time goes:
time: 330 us; the launch traced here: 328 us
  starting transfers between devices  121 us (37%)
  waiting for transfers between devices  121 us (37%)
  matrix products  39.9 us (12%)
  local copies, waits for them, and re-layouts  19.9 us (6%)
  between operations  17.2 us (5%)
  blocking collectives  6.32 us (2%)
    ppermute x18, starting transfers between devices, extended_2(): lax.ppermute(tail, axis, [(i, (i + 1) % count) for i in range(ends)])  96.9 us
    unnamed x2, waiting for transfers between devices  89 us
    ppermute x18, waiting for transfers between devices, extended_2(): lax.ppermute(head, axis, [((i + 1) % count, i) for i in range(ends)])  31.5 us
    ppermute x18, starting transfers between devices, extended_2(): lax.ppermute(head, axis, [((i + 1) % count, i) for i in range(ends)])  23.7 us
    dot_general x20, matrix products, block_product(): return jnp.einsum('nab,nbk->nak', matrices, field, precision=precise)  22.2 us
    dot_general x18, matrix products, coupled(): return jnp.einsum('nsab,nsbk->nak', coupling, picked, precision=precise)  16.8 us
    gather x18, local copies, waits for them, and re-layouts, coupled(): picked = jnp.take(extended, local_col, axis=0)  12.2 us
  transfers between devices with their start and end apart: 37, of which 18 were waited for; matrix products, arithmetic and copies ran while one was open for 1% of the time, Pallas kernels for 0%

commit v1 on v0

v1 whole, which is shorter than its diff:
```python
import functools

import jax
import jax.numpy as jnp
from jax import lax
from jax.experimental import pallas as pl
from jax.experimental.pallas import tpu as pltpu
from jax.sharding import PartitionSpec as P

SWEEPS = 8
SLOTS = 2 * (SWEEPS + 1)
OFFSETS = (-2, -1, 1, 2)
LANES = 128
E_MATRIX = 2
f32, bf16 = jnp.float32, jnp.bfloat16
NEAR, FAR = 0, 1


def split(x):
    high = x.astype(bf16)
    return high, (x - high.astype(f32)).astype(bf16)


def beside(x):
    return jnp.concatenate(split(x), axis=1)


def below(x):
    return jnp.concatenate(split(x), axis=0)


def product(matrix, field):
    whole = jnp.dot(matrix, field, preferred_element_type=f32)
    rows, cols = whole.shape[0] // 2, whole.shape[1] // 2
    return (whole[:rows, :cols] + whole[:rows, cols:]) + (whole[rows:, :cols] + whole[rows:, cols:])


def kernel(
    count, others, size,
    rhs_ref, zo_ref, e_diag_ref, a_off_ref, e_off_ref, col_ref, inv_ref, shift_ref,
    res_ref, cross_ref,
    own, halo, pend, base, image, band, diag, local_m, halo_m, inverse, zot, partial, outbox, inbox,
    send_sem, recv_sem, cross_send, cross_recv,
):
    me = lax.axis_index("blk")
    mine = lax.axis_index("narrow")
    devices = count * others
    rank = me * others + mine
    parity = lax.rem(me, 2)
    halves = (1 - parity, parity)
    step_to = 1 - 2 * parity
    has_far = jnp.logical_and(me != 0, me != count - 1)
    near_id = me + step_to
    far_id = jnp.where(has_far, me - step_to, near_id)
    half_rows = 2 * size
    per = outbox.shape[2]

    barrier = pltpu.get_barrier_semaphore()

    def greet(d, carry):
        @pl.when(d != rank)
        def _():
            pl.semaphore_signal(
                barrier, inc=1,
                device_id={"blk": d // others, "narrow": lax.rem(d, others)},
                device_id_type=pl.DeviceIdType.MESH,
            )
        return carry

    lax.fori_loop(0, devices, greet, 0)

    @pl.when(jnp.logical_not(has_far))
    def _():
        def clear(s, carry):
            halo[s, FAR] = jnp.zeros((half_rows, LANES), f32)
            return carry
        lax.fori_loop(0, SLOTS, clear, 0)

    def copy_of(slot, side):
        return pltpu.make_async_remote_copy(
            src_ref=own.at[slot, halves[side]],
            dst_ref=halo.at[slot, side],
            send_sem=send_sem.at[slot, side],
            recv_sem=recv_sem.at[slot, side],
            device_id={"blk": near_id if side == NEAR else far_id},
            device_id_type=pl.DeviceIdType.MESH,
        )

    def send(slot, side):
        if side == NEAR:
            copy_of(slot, side).start()
        else:
            @pl.when(has_far)
            def _():
                copy_of(slot, side).start()

    def arrive(slot, side):
        if side == NEAR:
            copy_of(slot, side).wait_recv()
        else:
            @pl.when(has_far)
            def _():
                copy_of(slot, side).wait_recv()

    filler = jnp.zeros((LANES - size, 2 * LANES), bf16)

    def field(pieces):
        parts = []
        for piece in pieces:
            for b in range(2):
                parts += [beside(piece[b * size:(b + 1) * size]), filler]
        return jnp.concatenate(parts, axis=0)

    def solved(which, half, value):
        return jnp.concatenate(
            [product(inverse[which, half * 2 + b], beside(value[b * size:(b + 1) * size])) for b in range(2)], axis=0
        )

    def place(which, row, blocks):
        empty = jnp.zeros((size, LANES), bf16)
        half = row // 2
        for c in range(-2, 6):
            high, low = split(blocks[c - row]) if c - row in blocks else (empty, empty)
            if 0 <= c < 4:
                lanes = slice(c * LANES, (c + 1) * LANES)
                local_m[which, row * size:(row + 1) * size, lanes] = high
                local_m[which, (4 + row) * size:(5 + row) * size, lanes] = low
            elif (c < 0) == (half == 0):
                k = c + 2 if c < 0 else c - 4
                at = row - 2 * half
                lanes = slice(k * LANES, (k + 1) * LANES)
                halo_m[which, half, at * size:(at + 1) * size, lanes] = high
                halo_m[which, half, (2 + at) * size:(3 + at) * size, lanes] = low

    def build_bands():
        band[...] = jnp.zeros_like(band)
        diag[...] = jnp.zeros_like(diag)
        for i in range(4):
            diag[i, :, 0:size] = e_diag_ref[i]
            for k, offset in enumerate(OFFSETS):
                total_a = jnp.zeros((size, size), f32)
                total_e = jnp.zeros((size, size), f32)
                for s in range(3):
                    weight = jnp.where(col_ref[i, s] == me * 4 + (i + offset), f32(1.0), f32(0.0))
                    total_a = total_a + weight * a_off_ref[i, s]
                    total_e = total_e + weight * e_off_ref[i, s]
                band[0, i, :, k * LANES:k * LANES + size] = total_a
                band[1, i, :, k * LANES:k * LANES + size] = total_e

    def build_sweep(which):
        q = shift_ref[which]
        for i in range(4):
            merged = product(inverse[which, i], beside(band[0, i] - q * band[1, i]))
            place(which, i, {o: merged[:, k * LANES:(k + 1) * LANES] for k, o in enumerate(OFFSETS)})

    def build_mass():
        for i in range(4):
            blocks = {o: band[1, i, :, k * LANES:(k + 1) * LANES] for k, o in enumerate(OFFSETS)}
            blocks[0] = diag[i]
            place(E_MATRIX, i, blocks)

    def inner(which, slot):
        return product(local_m[which], field([own[slot, 0], own[slot, 1]]))

    def outer(which, slot, side):
        arrive(slot, side)
        return product(halo_m[which, halves[side]], field([halo[slot, side]]))

    def sweep_inner(which, slot):
        got = inner(which, slot)
        for half in range(2):
            pend[half] = base[half] - got[half * half_rows:(half + 1) * half_rows]

    def sweep_outer(which, slot):
        for side in (NEAR, FAR):
            own[slot + 1, halves[side]] = pend[halves[side]] - outer(which, slot, side)
            send(slot + 1, side)

    for which in range(2):
        for i in range(4):
            inverse[which, i] = below(inv_ref[which, i])
    for half in range(2):
        value = rhs_ref[half * half_rows:(half + 1) * half_rows]
        start = solved(0, half, value)
        base[half] = start
        own[0, half] = start
    pl.semaphore_wait(barrier, devices - 1)
    send(0, FAR)
    send(0, NEAR)
    build_bands()
    build_sweep(0)

    ko = zo_ref.shape[1]
    for which in range(2):
        first = which * (SWEEPS + 1)
        q = shift_ref[which]
        sweep_inner(which, first)
        sweep_outer(which, first)
        done = 1
        if which == 0:
            sweep_inner(which, first + 1)
            build_mass()
            sweep_outer(which, first + 1)
            sweep_inner(which, first + 2)
            build_sweep(1)
            sweep_outer(which, first + 2)
            zot[...] = below(jnp.transpose(zo_ref[...]))
            done = 3

        def sweep(s, carry):
            sweep_inner(which, first + s)
            sweep_outer(which, first + s)
            return carry

        lax.fori_loop(done, SWEEPS, sweep, 0)

        last = first + SWEEPS
        got = inner(E_MATRIX, last)
        for half in range(2):
            pend[half] = got[half * half_rows:(half + 1) * half_rows]
        root = jnp.sqrt(jnp.full((1, LANES), 2.0 * q, f32))
        for side in (NEAR, FAR):
            half = halves[side]
            mass = pend[half] + outer(E_MATRIX, last, side)
            rows = pl.ds(pl.multiple_of(half * half_rows, 8), half_rows)
            before = rhs_ref[rows, :] if which == 0 else res_ref[rows, :]
            after = before + (2.0 * q) * mass
            res_ref[rows, :] = after
            image[half] = root * mass
            if which == 0:
                start = solved(1, half, after)
                base[half] = start
                own[last + 1, half] = start
                send(last + 1, side)

        pieces = jnp.concatenate([beside(image[0]), beside(image[1])], axis=0)
        partial[...] = product(zot[...], pieces)

        def pack(d, carry):
            outbox[which, d] = partial[pl.ds(d * per, per), :]
            return carry

        lax.fori_loop(0, devices, pack, 0)

        def post(d, carry):
            @pl.when(d != rank)
            def _():
                pltpu.make_async_remote_copy(
                    src_ref=outbox.at[which, d],
                    dst_ref=inbox.at[which, rank],
                    send_sem=cross_send.at[which],
                    recv_sem=cross_recv.at[which],
                    device_id={"blk": d // others, "narrow": lax.rem(d, others)},
                    device_id_type=pl.DeviceIdType.MESH,
                ).start()
            return carry

        lax.fori_loop(0, devices, post, 0)
        inbox[which, rank] = outbox[which, rank]

    for which in range(2):
        most = pl.ds(0, devices - 1)
        pltpu.make_async_copy(outbox.at[which, most], inbox.at[which, most], cross_recv.at[which]).wait()
        for n in range(others):
            total = inbox[which, n]
            for b in range(1, count):
                total = total + inbox[which, b * others + n]
            cross_ref[:, which, n * LANES:(n + 1) * LANES] = total
        pltpu.make_async_copy(outbox.at[which, most], inbox.at[which, most], cross_send.at[which]).wait()

    def settle(slot, carry):
        copy_of(slot, NEAR).wait_send()

        @pl.when(has_far)
        def _():
            copy_of(slot, FAR).wait_send()
        return carry

    lax.fori_loop(0, SLOTS, settle, 0)


def shards(count, others, rhs, zo, e_diag, a_off, e_off, col_index, inv_diag, shifts):
    row_count, col_width = rhs.shape
    size = e_diag.shape[1]
    ko = zo.shape[1]
    devices = count * others
    per = ko // devices
    half_rows = 2 * size
    assert row_count == 4 * size and col_width == LANES and count % 2 == 0
    vmem = pl.BlockSpec(memory_space=pltpu.VMEM)
    smem = pl.BlockSpec(memory_space=pltpu.SMEM)
    return pl.pallas_call(
        functools.partial(kernel, count, others, size),
        out_shape=(
            jax.ShapeDtypeStruct((row_count, col_width), f32),
            jax.ShapeDtypeStruct((per, 2, others * LANES), f32),
        ),
        in_specs=[vmem, vmem, vmem, vmem, vmem, smem, vmem, smem],
        out_specs=(vmem, vmem),
        scratch_shapes=[
            pltpu.VMEM((SLOTS, 2, half_rows, LANES), f32),
            pltpu.VMEM((SLOTS, 2, half_rows, LANES), f32),
            pltpu.VMEM((2, half_rows, LANES), f32),
            pltpu.VMEM((2, half_rows, LANES), f32),
            pltpu.VMEM((2, half_rows, LANES), f32),
            pltpu.VMEM((2, 4, size, 4 * LANES), f32),
            pltpu.VMEM((4, size, LANES), f32),
            pltpu.VMEM((3, 8 * size, 4 * LANES), bf16),
            pltpu.VMEM((3, 2, 4 * size, 2 * LANES), bf16),
            pltpu.VMEM((2, 4, 2 * size, size), bf16),
            pltpu.VMEM((2 * ko, row_count), bf16),
            pltpu.VMEM((ko, LANES), f32),
            pltpu.VMEM((2, devices, per, LANES), f32),
            pltpu.VMEM((2, devices, per, LANES), f32),
            pltpu.SemaphoreType.DMA((SLOTS, 2)),
            pltpu.SemaphoreType.DMA((SLOTS, 2)),
            pltpu.SemaphoreType.DMA((2,)),
            pltpu.SemaphoreType.DMA((2,)),
        ],
        compiler_params=pltpu.CompilerParams(collective_id=0, has_side_effects=True),
    )(rhs, zo, e_diag, a_off, e_off, col_index, inv_diag, shifts)


def solution(mesh):
    placed = (
        P("blk", "narrow"),
        P("blk", None),
        P("blk", None, None),
        P("blk", None, None, None),
        P("blk", None, None, None),
        P("blk", None),
        P(None, "blk", None, None),
        P(),
    )
    return jax.shard_map(
        functools.partial(shards, mesh.shape["blk"], mesh.shape["narrow"]),
        mesh=mesh,
        in_specs=placed,
        out_specs=(P("blk", "narrow"), P(("blk", "narrow"), None, None)),
        check_vma=False,
    )
```

time: 330 us -> 91.1 us (0.28)
  starting transfers between devices: 121 us -> 0 us
  waiting for transfers between devices: 121 us -> 0 us
  Pallas kernels: 0 us -> 86.3 us
  matrix products: 39.9 us -> 0 us
  between operations: 17.2 us -> 0.65 us
  local copies, waits for them, and re-layouts: 19.9 us -> 3.92 us
  blocking collectives: 6.32 us -> 0 us
    ppermute x36 -> x0, starting transfers between devices: 121 us -> none  [the longest x18 96.9 us: extended_2(): lax.ppermute(tail, axis, [(i, (i + 1) % count) for i in range(ends)])]
    unnamed x2 -> x0, waiting for transfers between devices: 89 us -> none
    pallas_call x0 -> x1, Pallas kernels: none -> 86.3 us  [shards(): pl.pallas_call(functools.partial(kernel, count, others, size), out_shape=...]
    dot_general x39 -> x0, matrix products: 39.9 us -> none  [the longest x20 22.2 us: block_product(): return jnp.einsum('nab,nbk->nak', matrices, field, precision=precise)]
    ppermute x36 -> x0, waiting for transfers between devices: 31.5 us -> none  [the longest x18 31.5 us: extended_2(): lax.ppermute(head, axis, [((i + 1) % count, i) for i in range(ends)])]
    gather x18 -> x0, local copies, waits for them, and re-layouts: 12.2 us -> none  [coupled(): picked = jnp.take(extended, local_col, axis=0)]
    all_to_all x1 -> x0, blocking collectives: 6.32 us -> none  [shards(): lax.all_to_all(summed, 'narrow', split_axis=0, concat_axis=2, tiled=True)]
  transfers between devices with their start and end apart: 37 -> 0, of which waited for: 18 -> 0; matrix products, arithmetic and copies ran while one was open for 1% -> 0% of each run, Pallas kernels for 0% -> 0%
where the time goes in v1:
time: 91.1 us; the launch traced here: 90.9 us
  Pallas kernels  86.3 us (95%)
  local copies, waits for them, and re-layouts  3.92 us (4%)
    pallas_call x1, Pallas kernels, shards(): pl.pallas_call(functools.partial(kernel, count, others, size), out_shape=...  86.3 us
    unnamed x5, local copies, waits for them, and re-layouts  3.92 us

profile of v1, /device:TPU:0, one launch (start us, length us, event | category | flops | bytes accessed | tf_op | source)
XLA Modules:
  0.0 90.9 jit_solution(4858618952276348113)
XLA Ops:
  0.6 1.7 %copy.10.zo_ref = f32[384,64]{1,0:T(8,128)} copy(f32[384,64]{0,1:T(8,128)} %param.9) | data formatting | bytes 196608 | tf_op args[1]
  2.3 86.3 %shard_map.95 = (f32[384,128]{1,0:T(8,128)}, f32[2,2,256]{2,1,0:T(2,128)}) custom-call(f32[384,128]{1,0:T(8,128)} %rhs_ref.1, f32[384,64]{1,0:T(8,128)} %copy.10.zo_ref, f32[4,96,96]{2,1,0:T(8,128)} %e_diag_ref.1, f32[4,3,96,96]{3,2,1,0:T(8,128)} %a_off_ref.1, f32[4,3,96,96]{3,2,1,0:T(8,128)} %e_off_ref.1, s32[4,3]{1,0:T(4,128)} %col_ref.1, ...), custom_call_target="tpu_custom_call" | custom-call | tf_op jit(solution)/shard_map/pallas_call | solution.py:292
  88.7 0.0 copy-start
  88.7 1.6 %copy.13 = f32[384,128]{1,0:T(8,128)} copy(f32[384,128]{1,0:T(8,128)} %get-tuple-element.4) | data formatting | bytes 393216
  90.3 0.0 copy-done
  90.3 0.6 copy.14
Async XLA Ops:
  88.7 1.6 %copy-start = (f32[2,2,256]{2,1,0:T(2,128)S(1)}, f32[2,2,256]{2,1,0:T(2,128)}, u32[]{:S(2)}) copy-start(f32[2,2,256]{2,1,0:T(2,128)} %get-tuple-element.5) | copy-start | bytes 12292

commit v2 on v1

v2 whole, which is shorter than its diff:
```python
import functools

import jax
import jax.numpy as jnp
from jax import lax
from jax.experimental import pallas as pl
from jax.experimental.pallas import tpu as pltpu
from jax.sharding import PartitionSpec as P

SWEEPS = 8
SLOTS = 2 * (SWEEPS + 1)
OFFSETS = (-2, -1, 1, 2)
LANES = 128
E_MATRIX = 2
f32, bf16 = jnp.float32, jnp.bfloat16
NEAR, FAR = 0, 1
EDGE, INNER = 0, 1


def split(x):
    high = x.astype(bf16)
    return high, (x - high.astype(f32)).astype(bf16)


def beside(x):
    return jnp.concatenate(split(x), axis=1)


def below(x):
    return jnp.concatenate(split(x), axis=0)


def product(matrix, field):
    whole = jnp.dot(matrix, field, preferred_element_type=f32)
    rows, cols = whole.shape[0] // 2, whole.shape[1] // 2
    return (whole[:rows, :cols] + whole[:rows, cols:]) + (whole[rows:, :cols] + whole[rows:, cols:])


def kernel(
    count, others, size,
    rhs_ref, zo_ref, e_diag_ref, a_off_ref, e_off_ref, col_ref, inv_ref, shift_ref,
    res_ref, cross_ref,
    own, halo, pend, base, image, band, diag, local_m, halo_m, inverse, zot, partial, outbox, inbox,
    send_sem, recv_sem, cross_send, cross_recv, tokens,
):
    me = lax.axis_index("blk")
    mine = lax.axis_index("narrow")
    devices = count * others
    rank = me * others + mine
    parity = lax.rem(me, 2)
    halves = (1 - parity, parity)
    step_to = 1 - 2 * parity
    has_far = jnp.logical_and(me != 0, me != count - 1)
    near_id = me + step_to
    far_id = jnp.where(has_far, me - step_to, near_id)
    per = outbox.shape[2]

    barrier = pltpu.get_barrier_semaphore()

    short = count <= SLOTS - 1

    def greet(**where):
        pl.semaphore_signal(barrier, inc=1, device_id=where, device_id_type=pl.DeviceIdType.MESH)

    def everyone(act):
        def at(b, carry):
            for n in range(others):
                @pl.when(jnp.logical_or(b != me, n != mine))
                def _():
                    act(b, n)
            return carry
        lax.fori_loop(0, count, at, 0)

    if short:
        greet(blk=near_id)

        @pl.when(has_far)
        def _():
            greet(blk=far_id)

        for k in range(1, others):
            greet(narrow=lax.rem(mine + k, others))
        greeted = others + jnp.where(has_far, 1, 0)
    else:
        everyone(lambda b, n: greet(blk=b, narrow=n))
        greeted = devices - 1

    @pl.when(jnp.logical_not(has_far))
    def _():
        def clear(s, carry):
            halo[s, FAR] = jnp.zeros((2, size, LANES), f32)
            return carry
        lax.fori_loop(0, SLOTS, clear, 0)

    def block_of(side, piece):
        return 3 * halves[side] if piece == EDGE else 1 + halves[side]

    def copy_of(slot, side, piece):
        return pltpu.make_async_remote_copy(
            src_ref=own.at[slot, block_of(side, piece)],
            dst_ref=halo.at[slot, side, piece],
            send_sem=send_sem.at[slot, side, piece],
            recv_sem=recv_sem.at[slot, side, piece],
            device_id={"blk": near_id if side == NEAR else far_id},
            device_id_type=pl.DeviceIdType.MESH,
        )

    def where_linked(side, act):
        if side == NEAR:
            act()
        else:
            pl.when(has_far)(act)

    def send(slot, side, piece):
        where_linked(side, lambda: copy_of(slot, side, piece).start())

    def arrive(slot, side, piece):
        where_linked(side, lambda: copy_of(slot, side, piece).wait_recv())

    filler = jnp.zeros((LANES - size, 2 * LANES), bf16)

    def field(blocks):
        parts = []
        for block in blocks:
            parts += [beside(block), filler]
        return jnp.concatenate(parts, axis=0)

    def solved(which, block, value):
        return product(inverse[which, block], beside(value))

    def place(which, row, blocks):
        empty = jnp.zeros((size, LANES), bf16)
        half = row // 2
        for c in range(-2, 6):
            high, low = split(blocks[c - row]) if c - row in blocks else (empty, empty)
            if 0 <= c < 4:
                lanes = slice(c * LANES, (c + 1) * LANES)
                local_m[which, row * size:(row + 1) * size, lanes] = high
                local_m[which, (4 + row) * size:(5 + row) * size, lanes] = low
            elif (c < 0) == (half == 0):
                k = EDGE if c in (-1, 4) else INNER
                at = EDGE if row in (0, 3) else INNER
                lanes = slice(k * LANES, (k + 1) * LANES)
                halo_m[which, half, 2 * at * size:(2 * at + 1) * size, lanes] = high
                halo_m[which, half, (2 * at + 1) * size:(2 * at + 2) * size, lanes] = low

    def build_bands():
        band[...] = jnp.zeros_like(band)
        diag[...] = jnp.zeros_like(diag)
        for i in range(4):
            diag[i, :, 0:size] = e_diag_ref[i]
            for k, offset in enumerate(OFFSETS):
                total_a = jnp.zeros((size, size), f32)
                total_e = jnp.zeros((size, size), f32)
                for s in range(3):
                    weight = jnp.where(col_ref[i, s] == me * 4 + (i + offset), f32(1.0), f32(0.0))
                    total_a = total_a + weight * a_off_ref[i, s]
                    total_e = total_e + weight * e_off_ref[i, s]
                band[0, i, :, k * LANES:k * LANES + size] = total_a
                band[1, i, :, k * LANES:k * LANES + size] = total_e

    def build_sweep(which):
        q = shift_ref[which]
        for i in range(4):
            merged = product(inverse[which, i], beside(band[0, i] - q * band[1, i]))
            place(which, i, {o: merged[:, k * LANES:(k + 1) * LANES] for k, o in enumerate(OFFSETS)})

    def build_mass():
        for i in range(4):
            blocks = {o: band[1, i, :, k * LANES:(k + 1) * LANES] for k, o in enumerate(OFFSETS)}
            blocks[0] = diag[i]
            place(E_MATRIX, i, blocks)

    def inner(which, slot):
        return product(local_m[which], field([own[slot, b] for b in range(4)]))

    def outer(which, slot, side, emit):
        part = 2 * size
        arrive(slot, side, EDGE)
        nearest = field([halo[slot, side, EDGE]])
        matrix = halo_m.at[which, halves[side]]
        emit(block_of(side, INNER), INNER, product(matrix[part:2 * part, 0:LANES], nearest))
        edge = product(matrix[0:part, 0:LANES], nearest)
        arrive(slot, side, INNER)
        edge = edge + product(matrix[0:part, LANES:2 * LANES], field([halo[slot, side, INNER]]))
        emit(block_of(side, EDGE), EDGE, edge)

    def pass_token(token, turn, target, slot):
        @pl.when(jnp.logical_and(turn == slot, turn > 0))
        def _():
            pl.semaphore_wait(tokens.at[token], 1)

        @pl.when(jnp.logical_and(turn == slot, turn < count - 1))
        def _():
            pl.semaphore_signal(
                tokens.at[token], inc=1, device_id={"blk": target}, device_id_type=pl.DeviceIdType.MESH
            )

    def pass_tokens(slot):
        if short:
            pass_token(0, me, jnp.minimum(me + 1, count - 1), slot)
            pass_token(1, count - 1 - me, jnp.maximum(me - 1, 0), slot)

    def sweep_inner(which, slot):
        pass_tokens(slot)
        got = inner(which, slot)
        for b in range(4):
            pend[b] = base[b] - got[b * size:(b + 1) * size]

    def sweep_outer(which, slot):
        for side in (NEAR, FAR):
            def emit(block, piece, value):
                own[slot + 1, block] = pend[block] - value
                send(slot + 1, side, piece)

            outer(which, slot, side, emit)

    for which in range(2):
        for i in range(4):
            inverse[which, i] = below(inv_ref[which, i])
    for b in range(4):
        start = solved(0, b, rhs_ref[b * size:(b + 1) * size])
        base[b] = start
        own[0, b] = start
    pl.semaphore_wait(barrier, greeted)
    for side in (FAR, NEAR):
        for piece in (EDGE, INNER):
            send(0, side, piece)
    build_bands()
    build_sweep(0)

    def post(which):
        def act(b, n):
            pltpu.make_async_remote_copy(
                src_ref=outbox.at[which, b * others + n],
                dst_ref=inbox.at[which, rank],
                send_sem=cross_send.at[which],
                recv_sem=cross_recv.at[which],
                device_id={"blk": b, "narrow": n},
                device_id_type=pl.DeviceIdType.MESH,
            ).start()

        everyone(act)

    for which in range(2):
        first = which * (SWEEPS + 1)
        q = shift_ref[which]
        sweep_inner(which, first)
        sweep_outer(which, first)
        done = 1
        if which == 0:
            sweep_inner(which, first + 1)
            build_mass()
            sweep_outer(which, first + 1)
            sweep_inner(which, first + 2)
            build_sweep(1)
            sweep_outer(which, first + 2)
            zot[...] = below(zo_ref[...])
            done = 3

        def sweep(s, carry):
            sweep_inner(which, first + s)
            sweep_outer(which, first + s)
            return carry

        lax.fori_loop(done, SWEEPS - which, sweep, 0)
        if which == 1:
            sweep_inner(which, first + SWEEPS - 1)
            post(0)
            sweep_outer(which, first + SWEEPS - 1)

        last = first + SWEEPS
        if which == 0:
            pass_tokens(last)
        got = inner(E_MATRIX, last)
        for b in range(4):
            pend[b] = got[b * size:(b + 1) * size]
        root = jnp.sqrt(jnp.full((1, LANES), 2.0 * q, f32))
        for side in (NEAR, FAR):
            def emit(block, piece, value):
                mass = pend[block] + value
                rows = pl.ds(pl.multiple_of(block * size, 8), size)
                before = rhs_ref[rows, :] if which == 0 else res_ref[rows, :]
                after = before + (2.0 * q) * mass
                res_ref[rows, :] = after
                image[block] = root * mass
                if which == 0:
                    start = solved(1, block, after)
                    base[block] = start
                    own[last + 1, block] = start
                    send(last + 1, side, piece)

            outer(E_MATRIX, last, side, emit)

        partial[...] = product(zot[...], jnp.concatenate([beside(image[b]) for b in range(4)], axis=0))

        def pack(d, carry):
            outbox[which, d] = partial[pl.ds(d * per, per), :]
            return carry

        lax.fori_loop(0, devices, pack, 0)

        if which == 1:
            post(1)
        inbox[which, rank] = outbox[which, rank]

    for which in range(2):
        most = pl.ds(0, devices - 1)
        pltpu.make_async_copy(outbox.at[which, most], inbox.at[which, most], cross_recv.at[which]).wait()
        for n in range(others):
            total = inbox[which, n]
            for b in range(1, count):
                total = total + inbox[which, b * others + n]
            cross_ref[:, which, n * LANES:(n + 1) * LANES] = total
        pltpu.make_async_copy(outbox.at[which, most], inbox.at[which, most], cross_send.at[which]).wait()

    def settle(slot, carry):
        for side in (NEAR, FAR):
            for piece in (EDGE, INNER):
                where_linked(side, lambda: copy_of(slot, side, piece).wait_send())
        return carry

    lax.fori_loop(0, SLOTS, settle, 0)


def shards(count, others, rhs, zo, e_diag, a_off, e_off, col_index, inv_diag, shifts):
    row_count, col_width = rhs.shape
    size = e_diag.shape[1]
    ko = zo.shape[1]
    devices = count * others
    per = ko // devices
    assert row_count == 4 * size and col_width == LANES and count % 2 == 0
    vmem = pl.BlockSpec(memory_space=pltpu.VMEM)
    smem = pl.BlockSpec(memory_space=pltpu.SMEM)
    return pl.pallas_call(
        functools.partial(kernel, count, others, size),
        out_shape=(
            jax.ShapeDtypeStruct((row_count, col_width), f32),
            jax.ShapeDtypeStruct((per, 2, others * LANES), f32),
        ),
        in_specs=[vmem, vmem, vmem, vmem, vmem, smem, vmem, smem],
        out_specs=(vmem, vmem),
        scratch_shapes=[
            pltpu.VMEM((SLOTS, 4, size, LANES), f32),
            pltpu.VMEM((SLOTS, 2, 2, size, LANES), f32),
            pltpu.VMEM((4, size, LANES), f32),
            pltpu.VMEM((4, size, LANES), f32),
            pltpu.VMEM((4, size, LANES), f32),
            pltpu.VMEM((2, 4, size, 4 * LANES), f32),
            pltpu.VMEM((4, size, LANES), f32),
            pltpu.VMEM((3, 8 * size, 4 * LANES), bf16),
            pltpu.VMEM((3, 2, 4 * size, 2 * LANES), bf16),
            pltpu.VMEM((2, 4, 2 * size, size), bf16),
            pltpu.VMEM((2 * ko, row_count), bf16),
            pltpu.VMEM((ko, LANES), f32),
            pltpu.VMEM((2, devices, per, LANES), f32),
            pltpu.VMEM((2, devices, per, LANES), f32),
            pltpu.SemaphoreType.DMA((SLOTS, 2, 2)),
            pltpu.SemaphoreType.DMA((SLOTS, 2, 2)),
            pltpu.SemaphoreType.DMA((2,)),
            pltpu.SemaphoreType.DMA((2,)),
            pltpu.SemaphoreType.REGULAR((2,)),
        ],
        compiler_params=pltpu.CompilerParams(collective_id=0, has_side_effects=True),
    )(rhs, zo.T, e_diag, a_off, e_off, col_index, inv_diag, shifts)


def solution(mesh):
    placed = (
        P("blk", "narrow"),
        P("blk", None),
        P("blk", None, None),
        P("blk", None, None, None),
        P("blk", None, None, None),
        P("blk", None),
        P(None, "blk", None, None),
        P(),
    )
    return jax.shard_map(
        functools.partial(shards, mesh.shape["blk"], mesh.shape["narrow"]),
        mesh=mesh,
        in_specs=placed,
        out_specs=(P("blk", "narrow"), P(("blk", "narrow"), None, None)),
        check_vma=False,
    )
```

time: 91.1 us -> 86.6 us (0.951)
  Pallas kernels: 86.3 us -> 83.6 us
  local copies, waits for them, and re-layouts: 3.92 us -> 2.21 us
    pallas_call x1, Pallas kernels: 86.3 us -> 83.6 us  [shards(): pl.pallas_call(functools.partial(kernel, count, others, size), out_shape=...]
    unnamed x5 -> x4, local copies, waits for them, and re-layouts: 3.92 us -> 2.21 us
where the time goes in v2:
time: 86.6 us; the launch traced here: 86.5 us
  Pallas kernels  83.6 us (97%)
  local copies, waits for them, and re-layouts  2.21 us (3%)
    pallas_call x1, Pallas kernels, shards(): pl.pallas_call(functools.partial(kernel, count, others, size), out_shape=...  83.6 us
    unnamed x4, local copies, waits for them, and re-layouts  2.21 us

profile of v2, /device:TPU:0, one launch (start us, length us, event | category | flops | bytes accessed | tf_op | source)
XLA Modules:
  0.0 86.5 jit_solution(14016487388506085396)
XLA Ops:
  0.6 83.6 %shard_map.95 = (f32[384,128]{1,0:T(8,128)}, f32[2,2,256]{2,1,0:T(2,128)}) custom-call(f32[384,128]{1,0:T(8,128)} %rhs_ref.1, f32[64,384]{1,0:T(8,128)} %bitcast.1, f32[4,96,96]{2,1,0:T(8,128)} %e_diag_ref.1, f32[4,3,96,96]{3,2,1,0:T(8,128)} %a_off_ref.1, f32[4,3,96,96]{3,2,1,0:T(8,128)} %e_off_ref.1, s32[4,3]{1,0:T(4,128)} %col_ref.1, ...), custom_call_target="tpu_custom_call" | custom-call | tf_op jit(solution)/shard_map/pallas_call | solution.py:335
  84.2 0.0 copy-start
  84.3 1.6 %copy.12 = f32[384,128]{1,0:T(8,128)} copy(f32[384,128]{1,0:T(8,128)} %get-tuple-element.4) | data formatting | bytes 393216
  85.9 0.0 copy-done
  85.9 0.6 copy.13
Async XLA Ops:
  84.2 1.6 %copy-start = (f32[2,2,256]{2,1,0:T(2,128)S(1)}, f32[2,2,256]{2,1,0:T(2,128)}, u32[]{:S(2)}) copy-start(f32[2,2,256]{2,1,0:T(2,128)} %get-tuple-element.5) | copy-start | bytes 12292

commit v3 on v2

--- a/solution.py
+++ b/solution.py
@@ -38,10 +38,11 @@
 
 def kernel(
     count, others, size,
-    rhs_ref, zo_ref, e_diag_ref, a_off_ref, e_off_ref, col_ref, inv_ref, shift_ref,
+    rhs_hbm, zo_hbm, e_diag_hbm, a_off_hbm, e_off_hbm, col_ref, inv_hbm, shift_ref,
     res_ref, cross_ref,
     own, halo, pend, base, image, band, diag, local_m, halo_m, inverse, zot, partial, outbox, inbox,
     send_sem, recv_sem, cross_send, cross_recv, tokens,
+    rhs_ref, zo_ref, e_diag_ref, a_off_ref, e_off_ref, inv_ref, load_sem,
 ):
     me = lax.axis_index("blk")
     mine = lax.axis_index("narrow")
@@ -55,7 +56,16 @@
     far_id = jnp.where(has_far, me - step_to, near_id)
     per = outbox.shape[2]
 
+    loads = [
+        pltpu.make_async_copy(source, target, load_sem.at[k])
+        for k, (source, target) in enumerate((
+            (rhs_hbm, rhs_ref), (inv_hbm, inv_ref), (a_off_hbm, a_off_ref), (e_off_hbm, e_off_ref),
+            (e_diag_hbm, e_diag_ref), (zo_hbm, zo_ref),
+        ))
+    ]
     barrier = pltpu.get_barrier_semaphore()
+    for load in loads:
+        load.start()
 
     short = count <= SLOTS - 1
 
@@ -63,7 +73,8 @@
         pl.semaphore_signal(barrier, inc=1, device_id=where, device_id_type=pl.DeviceIdType.MESH)
 
     def everyone(act):
-        def at(b, carry):
+        def at(k, carry):
+            b = lax.rem(k + me + count // 2, count)
             for n in range(others):
                 @pl.when(jnp.logical_or(b != me, n != mine))
                 def _():
@@ -215,9 +226,10 @@
 
             outer(which, slot, side, emit)
 
-    for which in range(2):
-        for i in range(4):
-            inverse[which, i] = below(inv_ref[which, i])
+    loads[0].wait()
+    loads[1].wait()
+    for i in range(4):
+        inverse[0, i] = below(inv_ref[0, i])
     for b in range(4):
         start = solved(0, b, rhs_ref[b * size:(b + 1) * size])
         base[b] = start
@@ -226,8 +238,12 @@
     for side in (FAR, NEAR):
         for piece in (EDGE, INNER):
             send(0, side, piece)
+    for load in loads[2:]:
+        load.wait()
     build_bands()
     build_sweep(0)
+    for i in range(4):
+        inverse[1, i] = below(inv_ref[1, i])
 
     def post(which):
         def act(b, n):
@@ -298,7 +314,7 @@
             outbox[which, d] = partial[pl.ds(d * per, per), :]
             return carry
 
-        lax.fori_loop(0, devices, pack, 0)
+        lax.fori_loop(0, devices, pack, 0, unroll=8)
 
         if which == 1:
             post(1)
@@ -332,13 +348,14 @@
     assert row_count == 4 * size and col_width == LANES and count % 2 == 0
     vmem = pl.BlockSpec(memory_space=pltpu.VMEM)
     smem = pl.BlockSpec(memory_space=pltpu.SMEM)
+    hbm = pl.BlockSpec(memory_space=pl.ANY)
     return pl.pallas_call(
         functools.partial(kernel, count, others, size),
         out_shape=(
             jax.ShapeDtypeStruct((row_count, col_width), f32),
             jax.ShapeDtypeStruct((per, 2, others * LANES), f32),
         ),
-        in_specs=[vmem, vmem, vmem, vmem, vmem, smem, vmem, smem],
+        in_specs=[hbm, hbm, hbm, hbm, hbm, smem, hbm, smem],
         out_specs=(vmem, vmem),
         scratch_shapes=[
             pltpu.VMEM((SLOTS, 4, size, LANES), f32),
@@ -360,6 +377,8 @@
             pltpu.SemaphoreType.DMA((2,)),
             pltpu.SemaphoreType.DMA((2,)),
             pltpu.SemaphoreType.REGULAR((2,)),
+            *(pltpu.VMEM(x.shape, f32) for x in (rhs, zo.T, e_diag, a_off, e_off, inv_diag)),
+            pltpu.SemaphoreType.DMA((6,)),
         ],
         compiler_params=pltpu.CompilerParams(collective_id=0, has_side_effects=True),
     )(rhs, zo.T, e_diag, a_off, e_off, col_index, inv_diag, shifts)

time: 86.6 us -> 86.1 us (level)
  no operation moved by 1% of the time
where the time goes in v3:
time: 86.1 us; the launch traced here: 85.9 us
  Pallas kernels  83.1 us (97%)
  local copies, waits for them, and re-layouts  2.21 us (3%)
    pallas_call x1, Pallas kernels, shards(): pl.pallas_call(functools.partial(kernel, count, others, size), out_shape=...  83.1 us
    unnamed x4, local copies, waits for them, and re-layouts  2.21 us

profile of v3, /device:TPU:0, one launch (start us, length us, event | category | flops | bytes accessed | tf_op | source)
XLA Modules:
  0.0 85.9 jit_solution(2083313522687977779)
XLA Ops:
  0.6 83.1 %shard_map.95 = (f32[384,128]{1,0:T(8,128)}, f32[2,2,256]{2,1,0:T(2,128)}) custom-call(f32[384,128]{1,0:T(8,128)} %rhs_hbm.1, f32[64,384]{1,0:T(8,128)} %bitcast.1, f32[4,96,96]{2,1,0:T(8,128)} %e_diag_hbm.1, f32[4,3,96,96]{3,2,1,0:T(8,128)} %a_off_hbm.1, f32[4,3,96,96]{3,2,1,0:T(8,128)} %e_off_hbm.1, s32[4,3]{1,0:T(4,128)} %col_ref.1, ...), custom_call_target="tpu_custom_call" | custom-call | tf_op jit(solution)/shard_map/pallas_call | solution.py:352
  83.7 0.0 copy-start
  83.7 1.6 %copy.12 = f32[384,128]{1,0:T(8,128)} copy(f32[384,128]{1,0:T(8,128)} %get-tuple-element.4) | data formatting | bytes 393216
  85.3 0.0 copy-done
  85.4 0.6 copy.13
Async XLA Ops:
  83.7 1.6 %copy-start = (f32[2,2,256]{2,1,0:T(2,128)S(1)}, f32[2,2,256]{2,1,0:T(2,128)}, u32[]{:S(2)}) copy-start(f32[2,2,256]{2,1,0:T(2,128)} %get-tuple-element.5) | copy-start | bytes 12292
